TPU v7x, 32 devices: a whole 2x2x4 slice. The times are simulated.
32 devices in a mesh: imp: 8 (over z, y), camp: 4 (over x, core).
Axes of the slice: x: 2, y: 2, z: 4, core: 2. Of those that a mesh axis runs over, the one named last changes fastest.
Arguments:
- imp_emb: bfloat16 [16384, 256], P(('imp', 'camp')), may hold values from -512 to 512
- imp_cost: bfloat16 [16384], P(('imp', 'camp')), may hold values from 0.099609375 to 1
- camp_emb: bfloat16 [4096, 256], P(('camp', 'imp')), may hold values from -6 to 6
- prices: bfloat16 [4096], P(('camp', 'imp')), may hold values from -5 to 5
- spend_limits: float32 [4096], P(('camp', 'imp')), may hold values from 3 to 32
- block_lists: int32 [128, 4, 8], P('imp', 'camp'), may hold values from 0 to 7, as said below
- block_counts: int32 [128, 4], P('imp', 'camp'), may hold values from 1 to 8, as said below
Outputs:
- new_prices: float32 [4096], P(('camp', 'imp'))
- row_logz: float32 [16384], P('imp')
Inputs may be any that keep to these rules, and one draw needn't show every extreme that they name: `block_lists`: entries of a list of one tile and owner are distinct block numbers of that owner; slots past the count hold block numbers too, which are ignored. `block_counts`: tile 0 uses all 8 slots of every owner.
All inputs are finite; a program needn't handle non-finite values.
Results may differ from a plain program's by a relative error of at most 0.0003.
Values may be sent and summed in bfloat16 or wider, within the bound.
A program may use at most 64 MiB of HBM per device.

v0:
```python
import jax
import jax.numpy as jnp
from jax import lax
from jax.sharding import PartitionSpec as P

D = 256
BLOCK = 128
SLOTS = 8
GROUP = 4


def merged(array, axis, combine):
    everything = jax.tree.map(lambda part: lax.all_gather(part, axis), array)
    initial = jax.tree.map(lambda part: part[0], everything)

    def step(k, so_far):
        return combine(so_far, jax.tree.map(lambda part: part[k], everything))

    return lax.fori_loop(1, lax.axis_size(axis), step, initial)


def local(imp_emb, imp_cost, camp_emb, prices, spend_limits, block_lists, block_counts):
    scale = 3.0 / jnp.sqrt(jnp.float32(D))
    emb_rows, cost_rows = (
        lax.all_gather(imp_emb, "camp", axis=0, tiled=True),
        lax.all_gather(imp_cost, "camp", axis=0, tiled=True),
    )
    camp_all, price_all = (
        lax.all_gather(camp_emb, "imp", axis=0, tiled=True),
        lax.all_gather(prices, "imp", axis=0, tiled=True),
    )
    own_count = camp_all.shape[0] // BLOCK
    camp_table = camp_all.reshape(own_count, BLOCK, D)
    price_table = price_all.astype(jnp.float32).reshape(own_count, BLOCK)
    lists = block_lists[:, 0, :]
    counts = block_counts[:, 0]
    tiles = lists.shape[0]
    turns = tiles // GROUP
    emb_groups = emb_rows.reshape(turns, GROUP, BLOCK, D)
    cost_groups = cost_rows.astype(jnp.float32).reshape(turns, GROUP, BLOCK)
    list_groups = lists.reshape(turns, GROUP, SLOTS)
    count_groups = counts.reshape(turns, GROUP)

    def scores_of(emb, ids, cnt):
        chosen = camp_table[ids]
        chosen_price = price_table[ids]
        raw = jnp.einsum("gbd,gscd->gbsc", emb, chosen, preferred_element_type=jnp.float32)
        logits = raw * scale - chosen_price[:, None, :, :]
        live = (jnp.arange(SLOTS, dtype=jnp.int32)[None, :] < cnt[:, None])[:, None, :, None]
        return (logits, live)

    def local_both(items):
        emb, ids, cnt = items
        logits, live = scores_of(emb, ids, cnt)
        top_here = jnp.max(jnp.where(live, logits, -jnp.inf), axis=(2, 3))
        expo = jnp.exp(jnp.where(live, logits - top_here[:, :, None, None], -jnp.inf))
        return (top_here, jnp.sum(expo, axis=(2, 3)))

    tops_here, totals_here = lax.map(local_both, (emb_groups, list_groups, count_groups))

    def combine(first, second):
        larger = jnp.maximum(first[0], second[0])
        summed = first[1] * jnp.exp(first[0] - larger) + second[1] * jnp.exp(second[0] - larger)
        return (larger, summed)

    top, total = merged((tops_here, totals_here), "camp", combine)
    row_logz = (top + jnp.log(total)).reshape(tiles * BLOCK)
    block_index = jnp.arange(own_count, dtype=jnp.int32)

    def accumulate(spend, items):
        emb, ids, cnt, cost, top_now, total_now = items
        logits, live = scores_of(emb, ids, cnt)
        expo = jnp.exp(jnp.where(live, logits - top_now[:, :, None, None], -jnp.inf))
        weight = expo / total_now[:, :, None, None]
        contrib = jnp.sum(weight * cost[:, :, None, None], axis=1)
        slot_live = jnp.arange(SLOTS, dtype=jnp.int32)[None, :] < cnt[:, None]
        onehot = ((ids[:, :, None] == block_index[None, None, :]) & slot_live[:, :, None]).astype(
            jnp.float32
        )
        added = jnp.einsum("gso,gsc->oc", onehot, contrib, precision=lax.Precision.HIGHEST)
        return (spend + added, None)

    spend_zero = jnp.zeros((own_count, BLOCK), jnp.float32)
    spend, unused = lax.scan(
        accumulate, spend_zero, (emb_groups, list_groups, count_groups, cost_groups, top, total)
    )
    spend = spend.reshape(own_count * BLOCK)
    width = prices.shape[0]
    whole = lax.psum(spend, "imp")
    mine = lax.dynamic_slice_in_dim(whole, lax.axis_index("imp") * width, width)
    new_prices = prices.astype(jnp.float32) + 2.0 * (mine - spend_limits) / (mine + spend_limits)
    return (new_prices, row_logz)


def solution(mesh):
    return jax.shard_map(
        local,
        mesh=mesh,
        in_specs=(
            P(("imp", "camp"), None),
            P(("imp", "camp")),
            P(("camp", "imp"), None),
            P(("camp", "imp")),
            P(("camp", "imp")),
            P("imp", "camp", None),
            P("imp", "camp"),
        ),
        out_specs=(P(("camp", "imp")), P("imp")),
        check_vma=False,
    )
```

profile of v0, /device:TPU:0, one launch (start us, length us, event | category | flops | bytes accessed | tf_op | source)
XLA Modules:
  0.0 137.3 jit_solution(15288913521605371296)
XLA Ops:
  7.2 0.7 all-gather.6.cloned.1.call-update
  7.9 0.8 copy.12
  8.7 22.5 %all-gather.2 = bf16[8,1,128]{2,1,0:T(2,128)(2,1)S(1)} all-gather(bf16[1,1,128]{2,1,0:T(2,128)(2,1)} %bitcast.128), channel_id=1, replica_groups=mesh['imp'=8,'camp'=4] {'imp'}, dimensions={0}, use_global_device_ids=true | all-gather | bytes 2304 | tf_op jit(solution)/shard_map/all_gather | solution.py:30
  31.1 0.5 broadcast.122
  31.7 1.2 reduce.3
  32.9 0.1 reshape_squeeze.7
  33.0 0.7 reshape.223
  33.7 5.2 %all-gather.3 = bf16[4,1,512]{2,1,0:T(2,128)(2,1)S(1)} all-gather(bf16[1,1,512]{2,1,0:T(2,128)(2,1)S(1)} %reshape.223), channel_id=1, replica_groups=mesh['imp'=8,'camp'=4] {'camp'}, dimensions={0}, use_global_device_ids=true | all-gather | bytes 5120 | tf_op jit(solution)/shard_map/all_gather | solution.py:26
  38.9 31.4 %all_gather.25 = bf16[1024,256]{1,0:T(8,128)(2,1)S(1)} all-gather(bf16[128,256]{1,0:T(8,128)(2,1)} %param.15), channel_id=1, replica_groups=mesh['imp'=8,'camp'=4] {'imp'}, dimensions={0}, use_global_device_ids=true | all-gather | bytes 589824 | tf_op jit(solution)/shard_map/all_gather | solution.py:29
  70.3 16.5 %while.40 = (s32[]{:T(128)}, f32[4,4,128]{2,1,0:T(4,128)S(1)}, f32[4,4,128]{2,1,0:T(4,128)S(1)}, s32[4,4]{1,0:T(4,128)S(1)}, bf16[4,4,128,256]{3,2,1,0:T(8,128)(...) while((s32[]{:T(128)}, f32[4,4,128]{2,1,0:T(4,128)S(1)}, ...), condition=%wide.region_3.4_spmd, body=%wide.region_0.3_spmd.sunk | while | flops 273154176 | bytes 10833529 | solution.py:59
  70.3 0.1 reshape.264
  70.4 0.6 gather_fusion
  71.0 0.7 gather_fusion.1
  71.7 0.1 iota_compare_fusion.5
  71.7 1.9 %select_reduce_fusion.2 = (f32[4,128]{1,0:T(4,128)S(1)}, f32[4,128,8,128]{1,3,2,0:T(8,128)S(1)}) fusion(f32[4,8,128]{2,1,0:T(8,128)S(1)} %bitcast.117, pred[4,8]{1,0:T(4,128)(4,1)S(1)} %iota_compare_fusion.5, bf16[4,8,128,256]{3,2,1,0:T(8,128)(2,1)S(1)} %bitcast.116, bf16[4,4,128,256]{3,2,1,0:T(8,128)(2,1)} %get-tuple-element.508, ...), kind=kOutput, calls=%fused_computation.11.clone.1 | convolution fusion | flops 270532096 | bytes 4475424 | tf_op jit(solution)/shard_map/while/body/eval_jaxpr/gbd,gscd->gbsc/dot_general | solution.py:47
  73.6 0.8 exponential_reduce_fusion.2
  74.4 0.1 reshape.264
  74.5 0.6 gather_fusion
  75.1 0.7 gather_fusion.1
  75.8 0.1 iota_compare_fusion.5
  75.9 1.9 %select_reduce_fusion.2 = (f32[4,128]{1,0:T(4,128)S(1)}, f32[4,128,8,128]{1,3,2,0:T(8,128)S(1)}) fusion(f32[4,8,128]{2,1,0:T(8,128)S(1)} %bitcast.117, pred[4,8]{1,0:T(4,128)(4,1)S(1)} %iota_compare_fusion.5, bf16[4,8,128,256]{3,2,1,0:T(8,128)(2,1)S(1)} %bitcast.116, bf16[4,4,128,256]{3,2,1,0:T(8,128)(2,1)} %get-tuple-element.508, ...), kind=kOutput, calls=%fused_computation.11.clone.1 | convolution fusion | flops 270532096 | bytes 4475424 | tf_op jit(solution)/shard_map/while/body/eval_jaxpr/gbd,gscd->gbsc/dot_general | solution.py:47
  77.7 0.8 exponential_reduce_fusion.2
  78.6 0.1 reshape.264
  78.7 0.6 gather_fusion
  79.2 0.7 gather_fusion.1
  79.9 0.1 iota_compare_fusion.5
  80.0 1.9 %select_reduce_fusion.2 = (f32[4,128]{1,0:T(4,128)S(1)}, f32[4,128,8,128]{1,3,2,0:T(8,128)S(1)}) fusion(f32[4,8,128]{2,1,0:T(8,128)S(1)} %bitcast.117, pred[4,8]{1,0:T(4,128)(4,1)S(1)} %iota_compare_fusion.5, bf16[4,8,128,256]{3,2,1,0:T(8,128)(2,1)S(1)} %bitcast.116, bf16[4,4,128,256]{3,2,1,0:T(8,128)(2,1)} %get-tuple-element.508, ...), kind=kOutput, calls=%fused_computation.11.clone.1 | convolution fusion | flops 270532096 | bytes 4475424 | tf_op jit(solution)/shard_map/while/body/eval_jaxpr/gbd,gscd->gbsc/dot_general | solution.py:47
  81.9 0.8 exponential_reduce_fusion.2
  82.7 0.1 reshape.264
  82.8 0.6 gather_fusion
  83.4 0.7 gather_fusion.1
  84.1 0.1 iota_compare_fusion.5
  84.1 1.9 %select_reduce_fusion.2 = (f32[4,128]{1,0:T(4,128)S(1)}, f32[4,128,8,128]{1,3,2,0:T(8,128)S(1)}) fusion(f32[4,8,128]{2,1,0:T(8,128)S(1)} %bitcast.117, pred[4,8]{1,0:T(4,128)(4,1)S(1)} %iota_compare_fusion.5, bf16[4,8,128,256]{3,2,1,0:T(8,128)(2,1)S(1)} %bitcast.116, bf16[4,4,128,256]{3,2,1,0:T(8,128)(2,1)} %get-tuple-element.508, ...), kind=kOutput, calls=%fused_computation.11.clone.1 | convolution fusion | flops 270532096 | bytes 4475424 | tf_op jit(solution)/shard_map/while/body/eval_jaxpr/gbd,gscd->gbsc/dot_general | solution.py:47
  86.0 0.8 exponential_reduce_fusion.2
  86.8 5.2 %all-gather = f32[16,4,128]{2,1,0:T(4,128)S(1)} all-gather(f32[4,4,128]{2,1,0:T(4,128)S(1)} %get-tuple-element.235), channel_id=2, replica_groups=mesh['imp'=8,'camp'=4] {'camp'}, dimensions={0}, use_global_device_ids=true | all-gather | bytes 40960 | tf_op jit(solution)/shard_map/all_gather | solution.py:13
  92.0 5.2 %all-gather.1 = f32[16,4,128]{2,1,0:T(4,128)S(1)} all-gather(f32[4,4,128]{2,1,0:T(4,128)S(1)} %get-tuple-element.236), channel_id=3, replica_groups=mesh['imp'=8,'camp'=4] {'camp'}, dimensions={0}, use_global_device_ids=true | all-gather | bytes 40960 | tf_op jit(solution)/shard_map/all_gather | solution.py:13
  97.2 0.1 while.41
  97.3 14.7 %while.42 = (s32[]{:T(128)}, f32[8,128]{1,0:T(8,128)S(1)}, s32[4,4,8]{2,1,0:T(4,128)S(1)}, s32[4,4]{1,0:T(4,128)S(1)}, bf16[4,4,128,256]{3,2,1,0:T(8,128)(2,1)},...) while((s32[]{:T(128)}, f32[8,128]{1,0:T(8,128)S(1)}, ...), condition=%wide.region_8.9_spmd.clone, body=%wide.region_6.8_spmd.clone.sunk | while | flops 272498304 | bytes 6668323 | solution.py:84
  97.4 0.1 reshape.269
  97.5 0.7 gather_fusion.2
  98.2 0.6 gather_fusion.3
  98.8 0.1 iota_compare_fusion.6
  98.8 2.0 %multiply_reduce_fusion.2 = f32[4,8,128]{2,1,0:T(8,128)S(1)} fusion(bf16[4,8,128,256]{3,2,1,0:T(8,128)(2,1)S(1)} %bitcast.115, f32[4,128]{1,0:T(4,128)S(1)} %get-tuple-element.484, f32[4,128]{1,0:T(4,128)S(1)} %get-tuple-element.485, f32[4,128]{1,0:T(4,128)S(1)} %dynamic-slice_bitcast_fusion.8, f32[4,8,128]{2,1,0:T(8,128)S(1)} %bitcast.121, ...), kind=kOutput, calls=%fused_computation.24.clone.1 | convolution fusion | flops 272101376 | bytes 2398752 | tf_op jit(solution)/shard_map/while/body/eval_jaxpr/gbd,gscd->gbsc/dot_general | solution.py:47
  100.8 0.2 fusion.38
  101.0 0.1 reshape.269
  101.1 0.7 gather_fusion.2
  101.8 0.6 gather_fusion.3
  102.4 0.1 iota_compare_fusion.6
  102.5 2.0 %multiply_reduce_fusion.2 = f32[4,8,128]{2,1,0:T(8,128)S(1)} fusion(bf16[4,8,128,256]{3,2,1,0:T(8,128)(2,1)S(1)} %bitcast.115, f32[4,128]{1,0:T(4,128)S(1)} %get-tuple-element.484, f32[4,128]{1,0:T(4,128)S(1)} %get-tuple-element.485, f32[4,128]{1,0:T(4,128)S(1)} %dynamic-slice_bitcast_fusion.8, f32[4,8,128]{2,1,0:T(8,128)S(1)} %bitcast.121, ...), kind=kOutput, calls=%fused_computation.24.clone.1 | convolution fusion | flops 272101376 | bytes 2398752 | tf_op jit(solution)/shard_map/while/body/eval_jaxpr/gbd,gscd->gbsc/dot_general | solution.py:47
  104.5 0.2 fusion.38
  104.7 0.1 reshape.269
  104.8 0.7 gather_fusion.2
  105.5 0.6 gather_fusion.3
  106.2 2.0 %multiply_reduce_fusion.2 = f32[4,8,128]{2,1,0:T(8,128)S(1)} fusion(bf16[4,8,128,256]{3,2,1,0:T(8,128)(2,1)S(1)} %bitcast.115, f32[4,128]{1,0:T(4,128)S(1)} %get-tuple-element.484, f32[4,128]{1,0:T(4,128)S(1)} %get-tuple-element.485, f32[4,128]{1,0:T(4,128)S(1)} %dynamic-slice_bitcast_fusion.8, f32[4,8,128]{2,1,0:T(8,128)S(1)} %bitcast.121, ...), kind=kOutput, calls=%fused_computation.24.clone.1 | convolution fusion | flops 272101376 | bytes 2398752 | tf_op jit(solution)/shard_map/while/body/eval_jaxpr/gbd,gscd->gbsc/dot_general | solution.py:47
  108.2 0.2 fusion.38
  108.4 0.1 reshape.269
  108.5 0.7 gather_fusion.2
  109.2 0.6 gather_fusion.3
  109.8 0.1 iota_compare_fusion.6
  109.9 2.0 %multiply_reduce_fusion.2 = f32[4,8,128]{2,1,0:T(8,128)S(1)} fusion(bf16[4,8,128,256]{3,2,1,0:T(8,128)(2,1)S(1)} %bitcast.115, f32[4,128]{1,0:T(4,128)S(1)} %get-tuple-element.484, f32[4,128]{1,0:T(4,128)S(1)} %get-tuple-element.485, f32[4,128]{1,0:T(4,128)S(1)} %dynamic-slice_bitcast_fusion.8, f32[4,8,128]{2,1,0:T(8,128)S(1)} %bitcast.121, ...), kind=kOutput, calls=%fused_computation.24.clone.1 | convolution fusion | flops 272101376 | bytes 2398752 | tf_op jit(solution)/shard_map/while/body/eval_jaxpr/gbd,gscd->gbsc/dot_general | solution.py:47
  111.9 0.2 fusion.38
  112.1 17.2 %psum.7 = f32[1024]{0:T(1024)S(1)} all-reduce(f32[1024]{0:T(1024)S(1)} %bitcast.125), channel_id=1, replica_groups=mesh['imp'=8,'camp'=4] {'imp'}, use_global_device_ids=true, to_apply=%region_9.10 | all-reduce | flops 1024 | bytes 8192 | tf_op jit(solution)/shard_map/psum | solution.py:89
  129.3 0.6 log_add_fusion
  129.9 0.6 divide_add_fusion
  (57 shorter events, 0.6 us)
Async XLA Ops:
  7.2 63.1 %all-gather.6.cloned.1.call-start = ((), (), s32[]{:S(2)}) async-start(), calls=%async_computation | async-start | bytes 1310720 | tf_op jit(solution)/shard_map/all_gather | solution.py:25
  97.3 32.6 %copy-start = (bf16[128]{0:T(256)(128)(2,1)S(1)}, bf16[128]{0:T(256)(128)(2,1)}, u32[]{:S(2)}) copy-start(bf16[128]{0:T(256)(128)(2,1)} %param.16) | copy-start | bytes 772
  97.3 32.6 %copy-start.1 = (f32[128]{0:T(128)S(1)}, f32[128]{0:T(128)}, u32[]{:S(2)}) copy-start(f32[128]{0:T(128)} %param.17) | copy-start | bytes 1540
Sparse Core Ops, SparseCore 0:
  9.5 19.4 all-gather.5
where the time goes:
time: 138 us; the launch traced here: 137 us
  blocking collectives  86.6 us (63%)
  matrix products  16 us (12%)
  between operations  14.1 us (10%)
  local copies, waits for them, and re-layouts  13 us (9%)
  other arithmetic  6.35 us (5%)
    all_gather x1, blocking collectives, local(): lax.all_gather(camp_emb, 'imp', axis=0, tiled=True)  31.4 us
    all_gather x1, blocking collectives, local(): lax.all_gather(prices, 'imp', axis=0, tiled=True)  22.5 us
    psum x1, blocking collectives, local(): whole = lax.psum(spend, 'imp')  17.2 us
    dot_general x8, matrix products, scores_of(): jnp.einsum('gbd,gscd->gbsc', emb, chosen, preferred_element_type=jnp.floa...  15.3 us
    all_gather x2, blocking collectives, merged(): everything = jax.tree.map(lambda part: lax.all_gather(part, axis), array)  10.4 us
    gather x8, local copies, waits for them, and re-layouts, scores_of(): chosen = camp_table[ids]  5.48 us
    all_gather x1, blocking collectives, local(): lax.all_gather(imp_cost, 'camp', axis=0, tiled=True)  5.18 us
    gather x8, local copies, waits for them, and re-layouts, scores_of(): chosen_price = price_table[ids]  4.59 us
  transfers between devices with their start and end apart: 1, of which 0 were waited for; matrix products, arithmetic and copies ran while one was open for 2% of the time, Pallas kernels for 0%

commit v1 on v0

--- a/solution.py
+++ b/solution.py
@@ -7,6 +7,27 @@
 BLOCK = 128
 SLOTS = 8
 GROUP = 4
+
+
+def joined_along(pieces, dim):
+    shape = list(pieces.shape[1:])
+    shape[dim] *= pieces.shape[0]
+    return jnp.moveaxis(pieces, 0, dim).reshape(shape)
+
+
+def doubled(x, axis):
+    peers, mine = (lax.axis_size(axis), lax.axis_index(axis))
+    blocks, bit = (x[None], 1)
+    while bit < peers:
+        theirs = lax.ppermute(blocks, axis, [(i, i ^ bit) for i in range(peers)])
+        low = mine & bit == 0
+        blocks = jnp.concatenate([jnp.where(low, blocks, theirs), jnp.where(low, theirs, blocks)])
+        bit *= 2
+    return blocks
+
+
+def gather_by_bits(shard, axis, dim):
+    return joined_along(doubled(shard, axis), dim)
 
 
 def merged(array, axis, combine):
@@ -27,7 +48,7 @@
     )
     camp_all, price_all = (
         lax.all_gather(camp_emb, "imp", axis=0, tiled=True),
-        lax.all_gather(prices, "imp", axis=0, tiled=True),
+        gather_by_bits(prices, "imp", 0),
     )
     own_count = camp_all.shape[0] // BLOCK
     camp_table = camp_all.reshape(own_count, BLOCK, D)

time: 138 us -> 125 us (0.906)
  blocking collectives: 86.6 us -> 68.1 us
  starting transfers between devices: 0.04 us -> 4.33 us
    all_gather x1 -> x0, blocking collectives: 22.5 us -> none  [local(): lax.all_gather(prices, 'imp', axis=0, tiled=True)]
    ppermute x0 -> x3, starting transfers between devices: none -> 4.29 us  [doubled(): theirs = lax.ppermute(blocks, axis, [(i, i ^ bit) for i in range(peers)])]
    psum x1, blocking collectives: 17.2 us -> 20.3 us  [local(): whole = lax.psum(spend, 'imp')]
  transfers between devices with their start and end apart: 1 -> 4, of which waited for: 0 -> 1; matrix products, arithmetic and copies ran while one was open for 2% -> 3% of each run, Pallas kernels for 0% -> 0%
where the time goes in v1:
time: 125 us
  blocking collectives  68.1 us (54%)
  matrix products  16.1 us (13%)
  between operations  14.1 us (11%)
  local copies, waits for them, and re-layouts  13.1 us (10%)
  other arithmetic  7.16 us (6%)
  starting transfers between devices  4.33 us (3%)
  waiting for transfers between devices  1.29 us (1%)
    all_gather x1, blocking collectives, local(): lax.all_gather(camp_emb, 'imp', axis=0, tiled=True)  32.2 us
    psum x1, blocking collectives, local(): whole = lax.psum(spend, 'imp')  20.3 us
    dot_general x8, matrix products, scores_of(): jnp.einsum('gbd,gscd->gbsc', emb, chosen, preferred_element_type=jnp.floa...  15.3 us
    all_gather x2, blocking collectives, merged(): everything = jax.tree.map(lambda part: lax.all_gather(part, axis), array)  10.4 us
    gather x8, local copies, waits for them, and re-layouts, scores_of(): chosen = camp_table[ids]  5.48 us
    all_gather x1, blocking collectives, local(): lax.all_gather(imp_cost, 'camp', axis=0, tiled=True)  5.19 us
    gather x8, local copies, waits for them, and re-layouts, scores_of(): chosen_price = price_table[ids]  4.59 us
    ppermute x3, starting transfers between devices, doubled(): theirs = lax.ppermute(blocks, axis, [(i, i ^ bit) for i in range(peers)])  4.29 us
  transfers between devices with their start and end apart: 4, of which 1 were waited for; matrix products, arithmetic and copies ran while one was open for 3% of the time, Pallas kernels for 0%

profile of v1, /device:TPU:0, one launch (start us, length us, event | category | flops | bytes accessed | tf_op | source)
XLA Modules:
  0.0 124.6 jit_solution(13219708661366072794)
XLA Ops:
  7.2 0.7 all-gather.5.cloned.1.call-update
  7.9 3.1 %collective-permute-start = (bf16[1,128]{1,0:T(2,128)(2,1)}, bf16[1,128]{1,0:T(2,128)(2,1)S(1)}, u32[]{:S(2)}, u32[]{:S(2)}) collective-permute-start(bf16[1,128]{1,0:T(2,128)(2,1)} %bitcast.128), channel_id=1, source_target_pairs={{0,4},{4,0},{8,12},{12,8},{16,20},{20,16},{24,28},{28,24},{1,5},{5... | collective-permute-start | bytes 776 | tf_op jit(solution)/shard_map/ppermute | solution.py:22
  11.0 32.2 %all_gather.22 = bf16[1024,256]{1,0:T(8,128)(2,1)S(1)} all-gather(bf16[128,256]{1,0:T(8,128)(2,1)} %param.15), channel_id=1, replica_groups=mesh['imp'=8,'camp'=4] {'imp'}, dimensions={0}, use_global_device_ids=true | all-gather | bytes 589824 | tf_op jit(solution)/shard_map/all_gather | solution.py:50
  43.1 0.7 reshape.213
  43.8 0.7 broadcast_select_fusion.1
  44.5 5.2 %all-gather.2 = bf16[4,1,512]{2,1,0:T(2,128)(2,1)S(1)} all-gather(bf16[1,1,512]{2,1,0:T(2,128)(2,1)S(1)} %reshape.213), channel_id=1, replica_groups=mesh['imp'=8,'camp'=4] {'camp'}, dimensions={0}, use_global_device_ids=true | all-gather | bytes 5120 | tf_op jit(solution)/shard_map/all_gather | solution.py:47
  49.8 1.2 collective-permute-start.2
  50.9 0.8 copy.12
  51.7 0.6 broadcast.122
  52.3 1.4 %reduce.3 = s32[16]{0:T(128)S(1)} reduce(s32[16,1]{0,1:T(1,128)} %param.19, s32[]{:T(128)} %broadcast.122), dimensions={1}, to_apply=%param.19.reduce_sub_computation.3 | reduce | bytes 132 | tf_op args[6]
  53.6 0.1 reshape_squeeze.7
  53.7 0.6 collective-permute-done.2
  54.4 16.5 %while.40 = (s32[]{:T(128)}, f32[4,4,128]{2,1,0:T(4,128)S(1)}, f32[4,4,128]{2,1,0:T(4,128)S(1)}, s32[4,4]{1,0:T(4,128)S(1)}, bf16[4,4,128,256]{3,2,1,0:T(8,128)(...) while((s32[]{:T(128)}, f32[4,4,128]{2,1,0:T(4,128)S(1)}, ...), condition=%wide.region_3.4_spmd, body=%wide.region_0.3_spmd.sunk | while | flops 273154176 | bytes 10833529 | solution.py:80
  54.4 0.1 reshape.251
  54.5 0.6 gather_fusion
  55.1 0.7 gather_fusion.1
  55.8 0.1 iota_compare_fusion.5
  55.8 1.9 %select_reduce_fusion.2 = (f32[4,128]{1,0:T(4,128)S(1)}, f32[4,128,8,128]{1,3,2,0:T(8,128)S(1)}) fusion(f32[4,8,128]{2,1,0:T(8,128)S(1)} %bitcast.117, pred[4,8]{1,0:T(4,128)(4,1)S(1)} %iota_compare_fusion.5, bf16[4,8,128,256]{3,2,1,0:T(8,128)(2,1)S(1)} %bitcast.116, bf16[4,4,128,256]{3,2,1,0:T(8,128)(2,1)} %get-tuple-element.514, ...), kind=kOutput, calls=%fused_computation.11.clone.1 | convolution fusion | flops 270532096 | bytes 4475424 | tf_op jit(solution)/shard_map/while/body/eval_jaxpr/gbd,gscd->gbsc/dot_general | solution.py:68
  57.7 0.8 exponential_reduce_fusion.2
  58.5 0.1 reshape.251
  58.6 0.6 gather_fusion
  59.2 0.7 gather_fusion.1
  59.9 0.1 iota_compare_fusion.5
  60.0 1.9 %select_reduce_fusion.2 = (f32[4,128]{1,0:T(4,128)S(1)}, f32[4,128,8,128]{1,3,2,0:T(8,128)S(1)}) fusion(f32[4,8,128]{2,1,0:T(8,128)S(1)} %bitcast.117, pred[4,8]{1,0:T(4,128)(4,1)S(1)} %iota_compare_fusion.5, bf16[4,8,128,256]{3,2,1,0:T(8,128)(2,1)S(1)} %bitcast.116, bf16[4,4,128,256]{3,2,1,0:T(8,128)(2,1)} %get-tuple-element.514, ...), kind=kOutput, calls=%fused_computation.11.clone.1 | convolution fusion | flops 270532096 | bytes 4475424 | tf_op jit(solution)/shard_map/while/body/eval_jaxpr/gbd,gscd->gbsc/dot_general | solution.py:68
  61.8 0.8 exponential_reduce_fusion.2
  62.7 0.1 reshape.251
  62.8 0.6 gather_fusion
  63.3 0.7 gather_fusion.1
  64.0 0.1 iota_compare_fusion.5
  64.1 1.9 %select_reduce_fusion.2 = (f32[4,128]{1,0:T(4,128)S(1)}, f32[4,128,8,128]{1,3,2,0:T(8,128)S(1)}) fusion(f32[4,8,128]{2,1,0:T(8,128)S(1)} %bitcast.117, pred[4,8]{1,0:T(4,128)(4,1)S(1)} %iota_compare_fusion.5, bf16[4,8,128,256]{3,2,1,0:T(8,128)(2,1)S(1)} %bitcast.116, bf16[4,4,128,256]{3,2,1,0:T(8,128)(2,1)} %get-tuple-element.514, ...), kind=kOutput, calls=%fused_computation.11.clone.1 | convolution fusion | flops 270532096 | bytes 4475424 | tf_op jit(solution)/shard_map/while/body/eval_jaxpr/gbd,gscd->gbsc/dot_general | solution.py:68
  66.0 0.8 exponential_reduce_fusion.2
  66.8 0.1 reshape.251
  66.9 0.6 gather_fusion
  67.5 0.7 gather_fusion.1
  68.2 0.1 iota_compare_fusion.5
  68.2 1.9 %select_reduce_fusion.2 = (f32[4,128]{1,0:T(4,128)S(1)}, f32[4,128,8,128]{1,3,2,0:T(8,128)S(1)}) fusion(f32[4,8,128]{2,1,0:T(8,128)S(1)} %bitcast.117, pred[4,8]{1,0:T(4,128)(4,1)S(1)} %iota_compare_fusion.5, bf16[4,8,128,256]{3,2,1,0:T(8,128)(2,1)S(1)} %bitcast.116, bf16[4,4,128,256]{3,2,1,0:T(8,128)(2,1)} %get-tuple-element.514, ...), kind=kOutput, calls=%fused_computation.11.clone.1 | convolution fusion | flops 270532096 | bytes 4475424 | tf_op jit(solution)/shard_map/while/body/eval_jaxpr/gbd,gscd->gbsc/dot_general | solution.py:68
  70.1 0.8 exponential_reduce_fusion.2
  70.9 5.2 %all-gather = f32[16,4,128]{2,1,0:T(4,128)S(1)} all-gather(f32[4,4,128]{2,1,0:T(4,128)S(1)} %get-tuple-element.235), channel_id=2, replica_groups=mesh['imp'=8,'camp'=4] {'camp'}, dimensions={0}, use_global_device_ids=true | all-gather | bytes 40960 | tf_op jit(solution)/shard_map/all_gather | solution.py:34
  76.1 5.2 %all-gather.1 = f32[16,4,128]{2,1,0:T(4,128)S(1)} all-gather(f32[4,4,128]{2,1,0:T(4,128)S(1)} %get-tuple-element.236), channel_id=3, replica_groups=mesh['imp'=8,'camp'=4] {'camp'}, dimensions={0}, use_global_device_ids=true | all-gather | bytes 40960 | tf_op jit(solution)/shard_map/all_gather | solution.py:34
  81.3 0.1 while.41
  81.4 14.7 %while.42 = (s32[]{:T(128)}, f32[8,128]{1,0:T(8,128)S(1)}, s32[4,4,8]{2,1,0:T(4,128)S(1)}, s32[4,4]{1,0:T(4,128)S(1)}, bf16[4,4,128,256]{3,2,1,0:T(8,128)(2,1)},...) while((s32[]{:T(128)}, f32[8,128]{1,0:T(8,128)S(1)}, ...), condition=%wide.region_8.9_spmd.clone, body=%wide.region_6.8_spmd.clone.sunk | while | flops 272498304 | bytes 6668323 | solution.py:105
  81.5 0.1 reshape.256
  81.5 0.7 gather_fusion.2
  82.2 0.6 gather_fusion.3
  82.9 2.0 %multiply_reduce_fusion.2 = f32[4,8,128]{2,1,0:T(8,128)S(1)} fusion(bf16[4,8,128,256]{3,2,1,0:T(8,128)(2,1)S(1)} %bitcast.115, f32[4,128]{1,0:T(4,128)S(1)} %get-tuple-element.490, f32[4,128]{1,0:T(4,128)S(1)} %get-tuple-element.491, f32[4,128]{1,0:T(4,128)S(1)} %dynamic-slice_bitcast_fusion.8, f32[4,8,128]{2,1,0:T(8,128)S(1)} %bitcast.121, ...), kind=kOutput, calls=%fused_computation.24.clone.1 | convolution fusion | flops 272101376 | bytes 2398752 | tf_op jit(solution)/shard_map/while/body/eval_jaxpr/gbd,gscd->gbsc/dot_general | solution.py:68
  84.9 0.2 fusion.38
  85.1 0.1 reshape.256
  85.2 0.7 gather_fusion.2
  85.9 0.6 gather_fusion.3
  86.6 2.0 %multiply_reduce_fusion.2 = f32[4,8,128]{2,1,0:T(8,128)S(1)} fusion(bf16[4,8,128,256]{3,2,1,0:T(8,128)(2,1)S(1)} %bitcast.115, f32[4,128]{1,0:T(4,128)S(1)} %get-tuple-element.490, f32[4,128]{1,0:T(4,128)S(1)} %get-tuple-element.491, f32[4,128]{1,0:T(4,128)S(1)} %dynamic-slice_bitcast_fusion.8, f32[4,8,128]{2,1,0:T(8,128)S(1)} %bitcast.121, ...), kind=kOutput, calls=%fused_computation.24.clone.1 | convolution fusion | flops 272101376 | bytes 2398752 | tf_op jit(solution)/shard_map/while/body/eval_jaxpr/gbd,gscd->gbsc/dot_general | solution.py:68
  88.6 0.2 fusion.38
  88.8 0.1 reshape.256
  88.9 0.7 gather_fusion.2
  89.6 0.6 gather_fusion.3
  90.3 2.0 %multiply_reduce_fusion.2 = f32[4,8,128]{2,1,0:T(8,128)S(1)} fusion(bf16[4,8,128,256]{3,2,1,0:T(8,128)(2,1)S(1)} %bitcast.115, f32[4,128]{1,0:T(4,128)S(1)} %get-tuple-element.490, f32[4,128]{1,0:T(4,128)S(1)} %get-tuple-element.491, f32[4,128]{1,0:T(4,128)S(1)} %dynamic-slice_bitcast_fusion.8, f32[4,8,128]{2,1,0:T(8,128)S(1)} %bitcast.121, ...), kind=kOutput, calls=%fused_computation.24.clone.1 | convolution fusion | flops 272101376 | bytes 2398752 | tf_op jit(solution)/shard_map/while/body/eval_jaxpr/gbd,gscd->gbsc/dot_general | solution.py:68
  92.3 0.2 fusion.38
  92.5 0.1 reshape.256
  92.6 0.7 gather_fusion.2
  93.3 0.6 gather_fusion.3
  94.0 2.0 %multiply_reduce_fusion.2 = f32[4,8,128]{2,1,0:T(8,128)S(1)} fusion(bf16[4,8,128,256]{3,2,1,0:T(8,128)(2,1)S(1)} %bitcast.115, f32[4,128]{1,0:T(4,128)S(1)} %get-tuple-element.490, f32[4,128]{1,0:T(4,128)S(1)} %get-tuple-element.491, f32[4,128]{1,0:T(4,128)S(1)} %dynamic-slice_bitcast_fusion.8, f32[4,8,128]{2,1,0:T(8,128)S(1)} %bitcast.121, ...), kind=kOutput, calls=%fused_computation.24.clone.1 | convolution fusion | flops 272101376 | bytes 2398752 | tf_op jit(solution)/shard_map/while/body/eval_jaxpr/gbd,gscd->gbsc/dot_general | solution.py:68
  96.0 0.2 fusion.38
  96.2 20.3 %psum.7 = f32[1024]{0:T(1024)S(1)} all-reduce(f32[1024]{0:T(1024)S(1)} %bitcast.125), channel_id=1, replica_groups=mesh['imp'=8,'camp'=4] {'imp'}, use_global_device_ids=true, to_apply=%region_9.10 | all-reduce | flops 1024 | bytes 8192 | tf_op jit(solution)/shard_map/psum | solution.py:110
  116.5 0.6 log_add_fusion
  117.1 0.6 divide_add_fusion
  (67 shorter events, 0.9 us)
Async XLA Ops:
  7.2 47.2 %all-gather.5.cloned.1.call-start = ((), (), s32[]{:S(2)}) async-start(), calls=%async_computation | async-start | bytes 1310720 | tf_op jit(solution)/shard_map/all_gather | solution.py:46
  7.9 35.9 %collective-permute-start = (bf16[1,128]{1,0:T(2,128)(2,1)}, bf16[1,128]{1,0:T(2,128)(2,1)S(1)}, u32[]{:S(2)}, u32[]{:S(2)}) collective-permute-start(bf16[1,128]{1,0:T(2,128)(2,1)} %bitcast.128), channel_id=1, source_target_pairs={{0,4},{4,0},{8,12},{12,8},{16,20},{20,16},{24,28},{28,24},{1,5},{5... | collective-permute-start | bytes 776 | tf_op jit(solution)/shard_map/ppermute | solution.py:22
  44.5 5.3 %collective-permute-start.1 = (bf16[2,128]{1,0:T(2,128)(2,1)S(1)}, bf16[2,128]{1,0:T(2,128)(2,1)S(1)}, u32[]{:S(2)}, u32[]{:S(2)}) collective-permute-start(bf16[2,128]{1,0:T(2,128)(2,1)S(1)} %pad_maximum_fusion.1), channel_id=1, source_target_pairs={{0,8},{4,12},{8,0},{12,4},{16,24},{20,28},{24,16},{28,20},{1,9},{5... | collective-permute-start | bytes 1544 | tf_op jit(solution)/shard_map/ppermute | solution.py:22
  49.8 4.5 %collective-permute-start.2 = (bf16[4,128]{1,0:T(4,128)(2,1)S(1)}, bf16[4,128]{1,0:T(4,128)(2,1)S(1)}, u32[]{:S(2)}, u32[]{:S(2)}) collective-permute-start(bf16[4,128]{1,0:T(4,128)(2,1)S(1)} %pad_maximum_fusion), channel_id=1, source_target_pairs={{0,16},{4,20},{8,24},{12,28},{16,0},{20,4},{24,8},{28,12},{1,17},{... | collective-permute-start | bytes 3080 | tf_op jit(solution)/shard_map/ppermute | solution.py:22
  81.4 35.7 %copy-start = (bf16[128]{0:T(256)(128)(2,1)S(1)}, bf16[128]{0:T(256)(128)(2,1)}, u32[]{:S(2)}) copy-start(bf16[128]{0:T(256)(128)(2,1)} %param.16) | copy-start | bytes 772
  81.4 35.7 %copy-start.1 = (f32[128]{0:T(128)S(1)}, f32[128]{0:T(128)}, u32[]{:S(2)}) copy-start(f32[128]{0:T(128)} %param.17) | copy-start | bytes 1540
Sparse Core Ops, SparseCore 0:
  9.5 19.4 all-gather.4
